TPU v7x, 128 devices: a whole 4x4x4 slice. The times are simulated.
128 devices in a mesh: sx: 8 (over y, core), sy: 16 (over x, z).
Axes of the slice: x: 4, y: 4, z: 4, core: 2. Of those that a mesh axis runs over, the one named last changes fastest.
Arguments:
- loads: float32 [8, 16, 1536, 256], P('sx', 'sy')
- schur_flex: float32 [8, 16, 1536, 1536], P('sx', 'sy'), as said below
- dirichlet: float32 [8, 16, 1536, 1536], P('sx', 'sy'), as said below
- coupling: float32 [8, 16, 16, 1536], P('sx', 'sy'), may hold values from -0.3125 to 0.3125
- corner_index: int32 [8, 16, 16], P('sx', 'sy'), may hold values from 0 to 512, as said below
- face_lists: int32 [8, 16, 4, 384], P('sx', 'sy'), may hold values from 0 to 383, as said below
- coarse_inverse: float32 [512, 512], P(('sx', 'sy')), as said below
Outputs:
- multipliers: float32 [8, 16, 1536, 256], P('sx', 'sy')
- residual: float32 [8, 16, 1536, 256], P('sx', 'sy')
Inputs may be any that keep to these rules, and one draw needn't show every extreme that they name: `corner_index`: each subdomain lists 4 coarse dofs for each of its four corners; 512 marks a corner on the clamped edges of the panel, which has no coarse dof; every coarse dof below 512 is named by some subdomain. `face_lists`: each face's list is a permutation of the 384 dofs of the facing face; the facing lists of two neighbouring subdomains are inverse permutations. `schur_flex`: symmetric positive definite for every subdomain. `dirichlet`: symmetric positive definite for every subdomain. `coarse_inverse`: symmetric positive definite.
All inputs are finite; a program needn't handle non-finite values.
Results may differ from a plain program's by a relative error of at most 0.00017.
Values sent between devices are 32-bit elements; how exact they have to be, the bound alone decides.
A program may use at most 128 MiB of HBM per device.

v0:
```python
import jax
import jax.numpy as jnp
from jax import lax
from jax.sharding import PartitionSpec as P

ITERS = 2


def shifted(block, axis, distance):
    devices = range(lax.axis_size(axis))
    route = [(i - distance, i) for i in devices if i - distance in devices]
    return lax.ppermute(block, axis, route)


def jump(field, face_index):
    size = field.shape[0] // 4
    width = field.shape[1]
    face_rows = field.reshape(4, size, width)
    from_low_x = shifted(face_rows[1], "sx", 1)
    from_high_x = shifted(face_rows[0], "sx", -1)
    from_low_y = shifted(face_rows[3], "sy", 1)
    from_high_y = shifted(face_rows[2], "sy", -1)
    received = jnp.stack([from_low_x, from_high_x, from_low_y, from_high_y], axis=0)
    matched = received[jnp.arange(4, dtype=jnp.int32)[:, None], face_index]
    return (face_rows - matched).reshape(4 * size, width)


def coarse_solve(coarse_rhs, stiffness_inverse_lines):
    highest = lax.Precision.HIGHEST
    total = lax.psum(coarse_rhs, ("sx", "sy"))
    mine = jnp.dot(stiffness_inverse_lines, total, precision=highest)
    return lax.all_gather(mine, ("sx", "sy"), axis=0, tiled=True)


def inner(first, second):
    return jnp.sum(first * second, axis=0)


def shards(loads, schur_flex, dirichlet, coupling, corner_index, face_lists, coarse_inverse):
    high = lax.Precision.HIGH
    highest = lax.Precision.HIGHEST
    flex_mat = schur_flex[0, 0]
    prec_mat = dirichlet[0, 0]
    coupling_mat = coupling[0, 0]
    corners = corner_index[0, 0]
    face_index = face_lists[0, 0]
    ncoarse = coarse_inverse.shape[1]
    onehot = (corners[None, :] == jnp.arange(ncoarse, dtype=jnp.int32)[:, None]).astype(jnp.float32)
    size = face_index.shape[1]
    sx = lax.axis_index("sx")
    sy = lax.axis_index("sy")
    inside = jnp.stack([sx > 0, sx < lax.axis_size("sx") - 1, sy > 0, sy < lax.axis_size("sy") - 1])
    scale = jnp.repeat(1.0 + inside.astype(jnp.float32), size)[:, None]

    def total(values):
        return lax.psum(values, ("sx", "sy"))

    residual = jump(loads[0, 0], face_index)
    multipliers = jnp.zeros_like(residual)
    direction = None
    residual_inner = None
    for iteration in range(ITERS):
        spread = scale * residual
        operator_applied = jnp.dot(prec_mat, spread, precision=high)
        new_dot = total(0.5 * inner(spread, operator_applied))
        precond = 0.5 * jump(operator_applied, face_index)
        direction = precond if iteration == 0 else precond + new_dot / residual_inner * direction
        residual_inner = new_dot
        apply_spread = scale * direction
        fine_part = jnp.dot(flex_mat, apply_spread, precision=high)
        local_load = jnp.dot(coupling_mat, apply_spread, precision=high)
        coarse_rhs = jnp.dot(onehot, local_load, precision=highest)
        coarse_sol = coarse_solve(coarse_rhs, coarse_inverse)
        filled_out = jnp.concatenate(
            [coarse_sol, jnp.zeros((1, direction.shape[1]), jnp.float32)], axis=0
        )
        picked = filled_out[corners]
        correction = lax.dot_general(coupling_mat, picked, (((0,), (0,)), ((), ())), precision=high)
        applied = fine_part + correction
        step_size = residual_inner / total(inner(apply_spread, applied))
        image_dir = jump(applied, face_index)
        multipliers = multipliers + step_size * direction
        residual = residual - step_size * image_dir
    return (multipliers[None, None], residual[None, None])


def solution(mesh):
    return jax.shard_map(
        shards,
        mesh=mesh,
        in_specs=(
            P("sx", "sy", None, None),
            P("sx", "sy", None, None),
            P("sx", "sy", None, None),
            P("sx", "sy", None, None),
            P("sx", "sy", None),
            P("sx", "sy", None, None),
            P(("sx", "sy"), None),
        ),
        out_specs=(P("sx", "sy", None, None), P("sx", "sy", None, None)),
        check_vma=False,
    )
```

profile of v0, /device:TPU:1, one launch (start us, length us, event | category | flops | bytes accessed | tf_op | source)
XLA Modules:
  0.0 859.2 jit_solution(2950131900494569318)
XLA Ops:
  10.0 5.0 collective-permute-start.2
  17.9 3.2 collective-permute-start
  27.9 10.7 %gather_fusion = f32[1536,256]{1,0:T(8,128)S(1)} fusion(f32[4,384,256]{2,1,0:T(8,128)S(1)} %pad_maximum_fusion, s32[1536]{0:T(1024)S(1)} %reshape.131), kind=kCustom, calls=%fused_computation | custom fusion | bytes 3158016 | tf_op jit(solution)/shard_map/gather | solution.py:24
  38.6 11.8 %fusion.10 = f32[1536,256]{0,1:T(8,128)S(1)} fusion(f32[1,1,1536,1536]{3,2,1,0:T(8,128)} %param.9, f32[1,1,1536,256]{3,2,1,0:T(8,128)} %param.7, f32[1536,256]{1,0:T(8,128)S(1)} %gather_fusion, f32[1536]{0:T(1024)S(1)} %mul.105), kind=kOutput, calls=%fused_computation.19 | convolution fusion | flops 3624665088 | bytes 14161920 | tf_op jit(solution)/shard_map/dot_general | solution.py:64
  53.4 4.9 collective-permute-start.6
  60.2 4.8 collective-permute-start.4
  74.5 17.9 %gather_fusion.1 = f32[1536,256]{1,0:T(8,128)} fusion(f32[4,384,256]{2,1,0:T(8,128)S(1)} %copy.21, s32[1536]{0:T(1024)S(1)} %reshape.131), kind=kCustom, calls=%fused_computation.1 | custom fusion | bytes 3158016 | tf_op jit(solution)/shard_map/gather | solution.py:24
  92.4 3.1 copy.22
  100.6 6.7 fusion.2
  107.4 144.9 %all-reduce.6.cloned.1.call-done = f32[512,256]{1,0:T(8,128)} async-done(((f32[512,256]{1,0:T(8,128)}), f32[512,256]{1,0:T(8,128)}) %all-reduce.6.cloned.1.call-update) | async-done | bytes 524304 | tf_op jit(solution)/shard_map/psum | solution.py:30
  253.7 54.1 %all-gather = f32[128,4,256]{2,1,0:T(4,128)} all-gather(f32[1,4,256]{2,1,0:T(4,128)S(1)} %convolution_bitcast_fusion.1), channel_id=1, replica_groups=mesh['sx'=8,'sy'=16] {'sx','sy'}, dimensions={0}, use_global_device_ids=true | all-gather | bytes 528384 | tf_op jit(solution)/shard_map/all_gather | solution.py:32
  317.2 4.0 collective-permute-start.10
  323.7 3.1 collective-permute-start.8
  326.8 64.9 %all-reduce.2 = (f32[256]{0:T(256)S(1)}, f32[256]{0:T(256)S(1)}) all-reduce(f32[256]{0:T(256)S(1)} %broadcast_multiply_fusion.3, f32[256]{0:T(256)S(1)} %get-tuple-element.34), channel_id=1, replica_groups=mesh['sx'=8,'sy'=16] {'sx','sy'}, use_global_device_ids=true, to_apply=%region_1.0 | all-reduce | flops 512 | bytes 4096 | tf_op jit(solution)/shard_map/psum | solution.py:56
  396.0 17.9 %gather_fusion.3 = f32[1536,256]{1,0:T(8,128)} fusion(f32[4,384,256]{2,1,0:T(8,128)S(1)} %copy.25, s32[1536]{0:T(1024)S(1)} %reshape.131), kind=kCustom, calls=%fused_computation.3 | custom fusion | bytes 3158016 | tf_op jit(solution)/shard_map/gather | solution.py:24
  413.9 3.1 copy.26
  419.9 7.5 multiply_reduce_fusion.1
  430.2 4.0 collective-permute-start.14
  434.2 3.4 collective-permute-start.13
  439.8 65.1 %psum.45 = f32[256]{0:T(256)S(1)} all-reduce(f32[256]{0:T(256)S(1)} %broadcast_multiply_fusion.1), channel_id=1, replica_groups=mesh['sx'=8,'sy'=16] {'sx','sy'}, use_global_device_ids=true, to_apply=%region_6.0 | all-reduce | flops 256 | bytes 2048 | tf_op jit(solution)/shard_map/psum | solution.py:56
  509.3 17.9 %gather_fusion.4 = f32[1536,256]{1,0:T(8,128)} fusion(f32[4,384,256]{2,1,0:T(8,128)S(1)} %copy.27, s32[1536]{0:T(1024)S(1)} %reshape.131), kind=kCustom, calls=%fused_computation.4 | custom fusion | bytes 3158016 | tf_op jit(solution)/shard_map/gather | solution.py:24
  527.2 3.0 copy.28
  534.4 7.7 fusion
  542.2 134.3 %all-reduce.8.cloned.1.call-done = f32[512,256]{1,0:T(8,128)} async-done(((f32[512,256]{1,0:T(8,128)}), f32[512,256]{1,0:T(8,128)}) %all-reduce.8.cloned.1.call-update) | async-done | bytes 524304 | tf_op jit(solution)/shard_map/psum | solution.py:30
  677.9 54.1 %all-gather.1 = f32[128,4,256]{2,1,0:T(4,128)} all-gather(f32[1,4,256]{2,1,0:T(4,128)S(1)} %convolution_bitcast_fusion), channel_id=1, replica_groups=mesh['sx'=8,'sy'=16] {'sx','sy'}, dimensions={0}, use_global_device_ids=true | all-gather | bytes 528384 | tf_op jit(solution)/shard_map/all_gather | solution.py:32
  742.7 4.0 collective-permute-start.18
  749.2 3.1 collective-permute-start.16
  752.3 65.2 %psum.47 = f32[256]{0:T(256)S(1)} all-reduce(f32[256]{0:T(256)S(1)} %get-tuple-element.38), channel_id=1, replica_groups=mesh['sx'=8,'sy'=16] {'sx','sy'}, use_global_device_ids=true, to_apply=%region_9.0 | all-reduce | flops 256 | bytes 2048 | tf_op jit(solution)/shard_map/psum | solution.py:56
  821.8 17.9 %gather_fusion.6 = f32[1536,256]{1,0:T(8,128)} fusion(f32[4,384,256]{2,1,0:T(8,128)S(1)} %copy.29, s32[1536]{0:T(1024)S(1)} %reshape.131), kind=kCustom, calls=%fused_computation.6 | custom fusion | bytes 3158016 | tf_op jit(solution)/shard_map/gather | solution.py:24
  839.7 3.1 copy.30
  842.9 4.8 subtract_bitcast_fusion
  847.6 3.1 copy.31
  (117 shorter events, 85.9 us)
Async XLA Ops:
  7.2 91.2 %copy-start = (f32[1,1,16,1536]{3,2,1,0:T(8,128)S(1)}, f32[1,1,16,1536]{3,2,1,0:T(8,128)}, u32[]{:S(2)}) copy-start(f32[1,1,16,1536]{3,2,1,0:T(8,128)} %param.10) | copy-start | bytes 294916
  7.2 14.0 %copy-start.16 = (s32[1,1,4,384]{3,2,1,0:T(4,128)S(1)}, s32[1,1,4,384]{3,2,1,0:T(4,128)}, u32[]{:S(2)}) copy-start(s32[1,1,4,384]{3,2,1,0:T(4,128)} %param.12) | copy-start | bytes 18436
  7.2 245.1 %all-reduce.6.cloned.1.call-start = ((), (), s32[]{:S(2)}) async-start(), calls=%async_computation | async-start | bytes 1048576 | tf_op jit(solution)/shard_map/psum | solution.py:30
  8.7 13.2 %collective-permute-start.3 = (f32[384,256]{1,0:T(8,128)S(1)}, f32[384,256]{1,0:T(8,128)S(1)}, u32[]{:S(2)}, u32[]{:S(2)}) collective-permute-start(f32[384,256]{1,0:T(8,128)S(1)} %get-tuple-element.29), channel_id=1, source_target_pairs={{1,0},{2,1},{3,2},{4,3},{5,4},{6,5},{7,6},{8,7},{9,8},{10,9},{11,1... | collective-permute-start | bytes 1179656 | tf_op jit(solution)/shard_map/ppermute | solution.py:12
  10.0 12.8 %collective-permute-start.2 = (f32[384,256]{1,0:T(8,128)S(1)}, f32[384,256]{1,0:T(8,128)S(1)}, u32[]{:S(2)}, u32[]{:S(2)}) collective-permute-start(f32[384,256]{1,0:T(8,128)S(1)} %get-tuple-element.30), channel_id=1, source_target_pairs={{0,1},{1,2},{2,3},{3,4},{4,5},{5,6},{6,7},{7,8},{8,9},{9,10},{10,1... | collective-permute-start | bytes 1179656 | tf_op jit(solution)/shard_map/ppermute | solution.py:12
  15.0 9.6 %collective-permute-start.1 = (f32[384,256]{1,0:T(8,128)S(1)}, f32[384,256]{1,0:T(8,128)S(1)}, u32[]{:S(2)}, u32[]{:S(2)}) collective-permute-start(f32[384,256]{1,0:T(8,128)S(1)} %get-tuple-element.31), channel_id=1, source_target_pairs={{16,0},{32,16},{48,32},{64,48},{80,64},{96,80},{112,96},{17,1},{33... | collective-permute-start | bytes 1179656 | tf_op jit(solution)/shard_map/ppermute | solution.py:12
  17.9 7.9 collective-permute-start
  38.6 11.8 %copy-start.7 = (f32[1536,256]{1,0:T(8,128)}, f32[1536,256]{1,0:T(8,128)S(1)}, u32[]{:S(2)}) copy-start(f32[1536,256]{1,0:T(8,128)S(1)} %gather_fusion) | copy-start | bytes 4718596
  50.4 14.6 %copy-start.17 = (s32[1,1,16]{2,1,0:T(1,128)S(1)}, s32[1,1,16]{2,1,0:T(1,128)}, u32[]{:S(2)}) copy-start(s32[1,1,16]{2,1,0:T(1,128)} %param.11) | copy-start | bytes 196
  52.1 16.6 %collective-permute-start.7 = (f32[384,256]{0,1:T(8,128)}, f32[384,256]{0,1:T(8,128)}, u32[]{:S(2)}, u32[]{:S(2)}) collective-permute-start(f32[384,256]{0,1:T(8,128)} %get-tuple-element.25), channel_id=1, source_target_pairs={{1,0},{2,1},{3,2},{4,3},{5,4},{6,5},{7,6},{8,7},{9,8},{10,9},{11,1... | collective-permute-start | bytes 1179656 | tf_op jit(solution)/shard_map/ppermute | solution.py:12
  53.4 15.3 %collective-permute-start.6 = (f32[384,256]{0,1:T(8,128)}, f32[384,256]{0,1:T(8,128)}, u32[]{:S(2)}, u32[]{:S(2)}) collective-permute-start(f32[384,256]{0,1:T(8,128)} %get-tuple-element.26), channel_id=1, source_target_pairs={{0,1},{1,2},{2,3},{3,4},{4,5},{5,6},{6,7},{7,8},{8,9},{9,10},{10,1... | collective-permute-start | bytes 1179656 | tf_op jit(solution)/shard_map/ppermute | solution.py:12
  58.3 10.5 %collective-permute-start.5 = (f32[384,256]{0,1:T(8,128)}, f32[384,256]{0,1:T(8,128)}, u32[]{:S(2)}, u32[]{:S(2)}) collective-permute-start(f32[384,256]{0,1:T(8,128)} %get-tuple-element.27), channel_id=1, source_target_pairs={{16,0},{32,16},{48,32},{64,48},{80,64},{96,80},{112,96},{17,1},{33... | collective-permute-start | bytes 1179656 | tf_op jit(solution)/shard_map/ppermute | solution.py:12
  60.2 9.8 %collective-permute-start.4 = (f32[384,256]{0,1:T(8,128)}, f32[384,256]{0,1:T(8,128)}, u32[]{:S(2)}, u32[]{:S(2)}) collective-permute-start(f32[384,256]{0,1:T(8,128)} %get-tuple-element.24), channel_id=1, source_target_pairs={{0,16},{16,32},{32,48},{48,64},{64,80},{80,96},{96,112},{1,17},{17... | collective-permute-start | bytes 1179656 | tf_op jit(solution)/shard_map/ppermute | solution.py:12
  67.0 28.4 %copy-start.3 = (f32[1,1,1536,256]{2,3,1,0:T(8,128)}, f32[1,1,1536,256]{2,3,1,0:T(8,128)S(1)}, u32[]{:S(2)}) copy-start(f32[1,1,1536,256]{2,3,1,0:T(8,128)S(1)} %copy.23) | copy-start | bytes 4718596
  100.4 151.9 %copy-start.15 = (f32[4,512]{1,0:T(4,128)S(1)}, f32[4,512]{1,0:T(4,128)}, u32[]{:S(2)}) copy-start(f32[4,512]{1,0:T(4,128)} %param.13) | copy-start | bytes 24580
  100.4 576.1 %all-reduce.8.cloned.1.call-start = ((), (), s32[]{:S(2)}) async-start(), calls=%async_computation.1 | async-start | bytes 1048576 | tf_op jit(solution)/shard_map/psum | solution.py:30
  315.9 75.8 %collective-permute-start.11 = (f32[384,256]{0,1:T(8,128)}, f32[384,256]{0,1:T(8,128)S(1)}, u32[]{:S(2)}, u32[]{:S(2)}) collective-permute-start(f32[384,256]{0,1:T(8,128)} %get-tuple-element.21), channel_id=1, source_target_pairs={{1,0},{2,1},{3,2},{4,3},{5,4},{6,5},{7,6},{8,7},{9,8},{10,9},{11,1... | collective-permute-start | bytes 1179656 | tf_op jit(solution)/shard_map/ppermute | solution.py:12
  317.2 74.5 %collective-permute-start.10 = (f32[384,256]{0,1:T(8,128)}, f32[384,256]{0,1:T(8,128)S(1)}, u32[]{:S(2)}, u32[]{:S(2)}) collective-permute-start(f32[384,256]{0,1:T(8,128)} %get-tuple-element.22), channel_id=1, source_target_pairs={{0,1},{1,2},{2,3},{3,4},{4,5},{5,6},{6,7},{7,8},{8,9},{9,10},{10,1... | collective-permute-start | bytes 1179656 | tf_op jit(solution)/shard_map/ppermute | solution.py:12
  321.2 70.5 %collective-permute-start.9 = (f32[384,256]{0,1:T(8,128)S(1)}, f32[384,256]{0,1:T(8,128)}, u32[]{:S(2)}, u32[]{:S(2)}) collective-permute-start(f32[384,256]{0,1:T(8,128)S(1)} %get-tuple-element.23), channel_id=1, source_target_pairs={{16,0},{32,16},{48,32},{64,48},{80,64},{96,80},{112,96},{17,1},{33... | collective-permute-start | bytes 1179656 | tf_op jit(solution)/shard_map/ppermute | solution.py:12
  323.7 68.0 %collective-permute-start.8 = (f32[384,256]{0,1:T(8,128)S(1)}, f32[384,256]{0,1:T(8,128)}, u32[]{:S(2)}, u32[]{:S(2)}) collective-permute-start(f32[384,256]{0,1:T(8,128)S(1)} %get-tuple-element.20), channel_id=1, source_target_pairs={{0,16},{16,32},{32,48},{48,64},{64,80},{80,96},{96,112},{1,17},{17... | collective-permute-start | bytes 1179656 | tf_op jit(solution)/shard_map/ppermute | solution.py:12
  413.9 3.1 copy-start.4
  419.9 7.6 copy-start.10
  428.9 76.0 %collective-permute-start.15 = (f32[384,256]{0,1:T(8,128)}, f32[384,256]{0,1:T(8,128)S(1)}, u32[]{:S(2)}, u32[]{:S(2)}) collective-permute-start(f32[384,256]{0,1:T(8,128)} %get-tuple-element.15), channel_id=1, source_target_pairs={{1,0},{2,1},{3,2},{4,3},{5,4},{6,5},{7,6},{8,7},{9,8},{10,9},{11,1... | collective-permute-start | bytes 1179656 | tf_op jit(solution)/shard_map/ppermute | solution.py:12
  430.2 74.7 %collective-permute-start.14 = (f32[384,256]{0,1:T(8,128)}, f32[384,256]{0,1:T(8,128)S(1)}, u32[]{:S(2)}, u32[]{:S(2)}) collective-permute-start(f32[384,256]{0,1:T(8,128)} %get-tuple-element.16), channel_id=1, source_target_pairs={{0,1},{1,2},{2,3},{3,4},{4,5},{5,6},{6,7},{7,8},{8,9},{9,10},{10,1... | collective-permute-start | bytes 1179656 | tf_op jit(solution)/shard_map/ppermute | solution.py:12
  434.2 70.7 %collective-permute-start.13 = (f32[384,256]{0,1:T(8,128)S(1)}, f32[384,256]{0,1:T(8,128)}, u32[]{:S(2)}, u32[]{:S(2)}) collective-permute-start(f32[384,256]{0,1:T(8,128)S(1)} %get-tuple-element.17), channel_id=1, source_target_pairs={{16,0},{32,16},{48,32},{64,48},{80,64},{96,80},{112,96},{17,1},{33... | collective-permute-start | bytes 1179656 | tf_op jit(solution)/shard_map/ppermute | solution.py:12
  437.6 67.3 %collective-permute-start.12 = (f32[384,256]{0,1:T(8,128)S(1)}, f32[384,256]{0,1:T(8,128)}, u32[]{:S(2)}, u32[]{:S(2)}) collective-permute-start(f32[384,256]{0,1:T(8,128)S(1)} %get-tuple-element.14), channel_id=1, source_target_pairs={{0,16},{16,32},{32,48},{48,64},{64,80},{80,96},{96,112},{1,17},{17... | collective-permute-start | bytes 1179656 | tf_op jit(solution)/shard_map/ppermute | solution.py:12
  532.4 205.1 %copy-start.1 = (f32[1536,256]{0,1:T(8,128)}, f32[1536,256]{0,1:T(8,128)S(1)}, u32[]{:S(2)}) copy-start(f32[1536,256]{0,1:T(8,128)S(1)} %multiply_add_fusion) | copy-start | bytes 4718596
  741.4 76.0 %collective-permute-start.19 = (f32[384,256]{0,1:T(8,128)}, f32[384,256]{0,1:T(8,128)S(1)}, u32[]{:S(2)}, u32[]{:S(2)}) collective-permute-start(f32[384,256]{0,1:T(8,128)} %get-tuple-element.11), channel_id=1, source_target_pairs={{1,0},{2,1},{3,2},{4,3},{5,4},{6,5},{7,6},{8,7},{9,8},{10,9},{11,1... | collective-permute-start | bytes 1179656 | tf_op jit(solution)/shard_map/ppermute | solution.py:12
  742.7 74.8 %collective-permute-start.18 = (f32[384,256]{0,1:T(8,128)}, f32[384,256]{0,1:T(8,128)S(1)}, u32[]{:S(2)}, u32[]{:S(2)}) collective-permute-start(f32[384,256]{0,1:T(8,128)} %get-tuple-element.12), channel_id=1, source_target_pairs={{0,1},{1,2},{2,3},{3,4},{4,5},{5,6},{6,7},{7,8},{8,9},{9,10},{10,1... | collective-permute-start | bytes 1179656 | tf_op jit(solution)/shard_map/ppermute | solution.py:12
  746.7 70.7 %collective-permute-start.17 = (f32[384,256]{0,1:T(8,128)S(1)}, f32[384,256]{0,1:T(8,128)}, u32[]{:S(2)}, u32[]{:S(2)}) collective-permute-start(f32[384,256]{0,1:T(8,128)S(1)} %get-tuple-element.13), channel_id=1, source_target_pairs={{16,0},{32,16},{48,32},{64,48},{80,64},{96,80},{112,96},{17,1},{33... | collective-permute-start | bytes 1179656 | tf_op jit(solution)/shard_map/ppermute | solution.py:12
  749.2 68.3 %collective-permute-start.16 = (f32[384,256]{0,1:T(8,128)S(1)}, f32[384,256]{0,1:T(8,128)}, u32[]{:S(2)}, u32[]{:S(2)}) collective-permute-start(f32[384,256]{0,1:T(8,128)S(1)} %get-tuple-element.10), channel_id=1, source_target_pairs={{0,16},{16,32},{32,48},{48,64},{64,80},{80,96},{96,112},{1,17},{17... | collective-permute-start | bytes 1179656 | tf_op jit(solution)/shard_map/ppermute | solution.py:12
  847.6 3.1 copy-start.12
  (8 other events, 13.0 us)
Sparse Core Ops, SparseCore 0:
  100.5 151.7 all-reduce.5
  534.6 141.8 all-reduce.7
where the time goes:
time: 861 us; the launch traced here: 859 us
  blocking collectives  303 us (35%)
  waiting for transfers between devices  285 us (33%)
  local copies, waits for them, and re-layouts  130 us (15%)
  starting transfers between devices  58.1 us (7%)
  matrix products  44.1 us (5%)
  other arithmetic  24 us (3%)
  between operations  14.6 us (2%)
    psum x2, waiting for transfers between devices, coarse_solve(): total = lax.psum(coarse_rhs, ('sx', 'sy'))  279 us
    psum x3, blocking collectives, total(): return lax.psum(values, ('sx', 'sy'))  195 us
    all_gather x2, blocking collectives, coarse_solve(): return lax.all_gather(mine, ('sx', 'sy'), axis=0, tiled=True)  108 us
    gather x10, local copies, waits for them, and re-layouts, jump(): matched = received[jnp.arange(4, dtype=jnp.int32)[:, None], face_index]  96.4 us
    ppermute x20, starting transfers between devices, shifted(): return lax.ppermute(block, axis, route)  57.8 us
    dot_general x2, matrix products, shards(): operator_applied = jnp.dot(prec_mat, spread, precision=high)  19.4 us
  transfers between devices with their start and end apart: 22, of which 8 were waited for; matrix products, arithmetic and copies ran while one was open for 2% of the time, Pallas kernels for 0%

commit v1 on v0

--- a/solution.py
+++ b/solution.py
@@ -29,7 +29,16 @@
     highest = lax.Precision.HIGHEST
     total = lax.psum(coarse_rhs, ("sx", "sy"))
     mine = jnp.dot(stiffness_inverse_lines, total, precision=highest)
-    return lax.all_gather(mine, ("sx", "sy"), axis=0, tiled=True)
+    bind_slot = lambda local_x: jnp.concatenate(
+        lax.all_to_all(
+            jnp.stack([local_x] * lax.psum(1, axis_name=("sx", "sy")), axis=0),
+            axis_name=("sx", "sy"),
+            split_axis=0,
+            concat_axis=0,
+        ),
+        0,
+    )
+    return bind_slot(mine)
 
 
 def inner(first, second):

time: 861 us -> 796 us (0.925)
  blocking collectives: 303 us -> 195 us
  waiting for transfers between devices: 285 us -> 312 us
  starting transfers between devices: 58.1 us -> 73.4 us
    all_gather x2 -> x0, blocking collectives: 108 us -> none  [coarse_solve(): return lax.all_gather(mine, ('sx', 'sy'), axis=0, tiled=True)]
    psum x2, waiting for transfers between devices: 279 us -> 294 us  [coarse_solve(): total = lax.psum(coarse_rhs, ('sx', 'sy'))]
    all_to_all x0 -> x2, starting transfers between devices: none -> 14.5 us  [coarse_solve(): lax.all_to_all(jnp.stack([local_x] * lax.psum(1, axis_name=('sx', 'sy')),...]
    all_to_all x0 -> x2, waiting for transfers between devices: none -> 11.4 us  [coarse_solve(): lax.all_to_all(jnp.stack([local_x] * lax.psum(1, axis_name=('sx', 'sy')),...]
  transfers between devices with their start and end apart: 22 -> 24, of which waited for: 8 -> 10; matrix products, arithmetic and copies ran while one was open for 2% -> 2% of each run, Pallas kernels for 0% -> 0%
where the time goes in v1:
time: 796 us; the launch traced here: 794 us
  waiting for transfers between devices  312 us (39%)
  blocking collectives  195 us (24%)
  local copies, waits for them, and re-layouts  132 us (17%)
  starting transfers between devices  73.4 us (9%)
  matrix products  44.1 us (6%)
  other arithmetic  24 us (3%)
  between operations  14.6 us (2%)
    psum x2, waiting for transfers between devices, coarse_solve(): total = lax.psum(coarse_rhs, ('sx', 'sy'))  294 us
    psum x3, blocking collectives, total(): return lax.psum(values, ('sx', 'sy'))  195 us
    gather x10, local copies, waits for them, and re-layouts, jump(): matched = received[jnp.arange(4, dtype=jnp.int32)[:, None], face_index]  96.4 us
    ppermute x20, starting transfers between devices, shifted(): return lax.ppermute(block, axis, route)  58.6 us
    dot_general x2, matrix products, shards(): operator_applied = jnp.dot(prec_mat, spread, precision=high)  19.4 us
  transfers between devices with their start and end apart: 24, of which 10 were waited for; matrix products, arithmetic and copies ran while one was open for 2% of the time, Pallas kernels for 0%

profile of v1, /device:TPU:1, one launch (start us, length us, event | category | flops | bytes accessed | tf_op | source)
XLA Modules:
  0.0 794.0 jit_solution(6499109192745056895)
XLA Ops:
  10.0 5.0 collective-permute-start.2
  17.9 3.2 collective-permute-start
  27.9 10.7 %gather_fusion = f32[1536,256]{1,0:T(8,128)S(1)} fusion(f32[4,384,256]{2,1,0:T(8,128)S(1)} %pad_maximum_fusion, s32[1536]{0:T(1024)S(1)} %reshape.143), kind=kCustom, calls=%fused_computation | custom fusion | bytes 3158016 | tf_op jit(solution)/shard_map/gather | solution.py:24
  38.6 11.8 %fusion.10 = f32[1536,256]{0,1:T(8,128)S(1)} fusion(f32[1,1,1536,1536]{3,2,1,0:T(8,128)} %param.9, f32[1,1,1536,256]{3,2,1,0:T(8,128)} %param.7, f32[1536,256]{1,0:T(8,128)S(1)} %gather_fusion, f32[1536]{0:T(1024)S(1)} %mul.105), kind=kOutput, calls=%fused_computation.19 | convolution fusion | flops 3624665088 | bytes 14161920 | tf_op jit(solution)/shard_map/dot_general | solution.py:73
  53.4 4.9 collective-permute-start.6
  60.2 4.9 collective-permute-start.4
  74.6 18.0 %gather_fusion.1 = f32[1536,256]{1,0:T(8,128)} fusion(f32[4,384,256]{2,1,0:T(8,128)S(1)} %copy.9, s32[1536]{0:T(1024)S(1)} %reshape.143), kind=kCustom, calls=%fused_computation.1 | custom fusion | bytes 3158016 | tf_op jit(solution)/shard_map/gather | solution.py:24
  100.6 151.8 %all-reduce.6.cloned.1.call-done = f32[512,256]{1,0:T(8,128)} async-done(((f32[512,256]{1,0:T(8,128)}), f32[512,256]{1,0:T(8,128)}) %all-reduce.6.cloned.1.call-update) | async-done | bytes 524304 | tf_op jit(solution)/shard_map/psum | solution.py:30
  254.8 7.2 all-to-all-start
  262.2 6.7 fusion.2
  269.0 6.1 all-to-all-done
  284.4 4.0 collective-permute-start.10
  288.5 3.7 collective-permute-start.9
  294.4 64.6 %all-reduce.2 = (f32[256]{0:T(256)S(1)}, f32[256]{0:T(256)S(1)}) all-reduce(f32[256]{0:T(256)S(1)} %broadcast_multiply_fusion.3, f32[256]{0:T(256)S(1)} %get-tuple-element.32), channel_id=1, replica_groups=mesh['sx'=8,'sy'=16] {'sx','sy'}, use_global_device_ids=true, to_apply=%region_1.0 | all-reduce | flops 512 | bytes 4096 | tf_op jit(solution)/shard_map/psum | solution.py:65
  363.3 17.9 %gather_fusion.3 = f32[1536,256]{1,0:T(8,128)} fusion(f32[4,384,256]{2,1,0:T(8,128)S(1)} %copy.13, s32[1536]{0:T(1024)S(1)} %reshape.143), kind=kCustom, calls=%fused_computation.3 | custom fusion | bytes 3158016 | tf_op jit(solution)/shard_map/gather | solution.py:24
  381.2 3.1 copy.14
  387.2 7.5 multiply_reduce_fusion.1
  397.5 4.0 collective-permute-start.14
  401.5 3.4 collective-permute-start.13
  407.1 65.1 %psum.45 = f32[256]{0:T(256)S(1)} all-reduce(f32[256]{0:T(256)S(1)} %broadcast_multiply_fusion.1), channel_id=1, replica_groups=mesh['sx'=8,'sy'=16] {'sx','sy'}, use_global_device_ids=true, to_apply=%region_6.0 | all-reduce | flops 256 | bytes 2048 | tf_op jit(solution)/shard_map/psum | solution.py:65
  476.6 18.0 %gather_fusion.4 = f32[1536,256]{1,0:T(8,128)} fusion(f32[4,384,256]{2,1,0:T(8,128)S(1)} %copy.15, s32[1536]{0:T(1024)S(1)} %reshape.143), kind=kCustom, calls=%fused_computation.4 | custom fusion | bytes 3158016 | tf_op jit(solution)/shard_map/gather | solution.py:24
  501.7 142.4 %all-reduce.8.cloned.1.call-done = f32[512,256]{1,0:T(8,128)} async-done(((f32[512,256]{1,0:T(8,128)}), f32[512,256]{1,0:T(8,128)}) %all-reduce.8.cloned.1.call-update) | async-done | bytes 524304 | tf_op jit(solution)/shard_map/psum | solution.py:30
  646.4 7.2 all-to-all-start.1
  653.6 7.7 fusion
  661.4 5.3 all-to-all-done.1
  677.4 4.0 collective-permute-start.18
  681.4 3.7 collective-permute-start.17
  687.4 64.9 %psum.47 = f32[256]{0:T(256)S(1)} all-reduce(f32[256]{0:T(256)S(1)} %get-tuple-element.36), channel_id=1, replica_groups=mesh['sx'=8,'sy'=16] {'sx','sy'}, use_global_device_ids=true, to_apply=%region_9.0 | all-reduce | flops 256 | bytes 2048 | tf_op jit(solution)/shard_map/psum | solution.py:65
  756.6 17.9 %gather_fusion.6 = f32[1536,256]{1,0:T(8,128)} fusion(f32[4,384,256]{2,1,0:T(8,128)S(1)} %copy.17, s32[1536]{0:T(1024)S(1)} %reshape.143), kind=kCustom, calls=%fused_computation.6 | custom fusion | bytes 3158016 | tf_op jit(solution)/shard_map/gather | solution.py:24
  774.5 3.1 copy.18
  777.6 4.8 subtract_bitcast_fusion
  782.4 3.1 copy.19
  (121 shorter events, 93.2 us)
Async XLA Ops:
  7.2 91.5 %copy-start = (f32[1,1,16,1536]{3,2,1,0:T(8,128)S(1)}, f32[1,1,16,1536]{3,2,1,0:T(8,128)}, u32[]{:S(2)}) copy-start(f32[1,1,16,1536]{3,2,1,0:T(8,128)} %param.10) | copy-start | bytes 294916
  7.2 14.0 %copy-start.16 = (s32[1,1,4,384]{3,2,1,0:T(4,128)S(1)}, s32[1,1,4,384]{3,2,1,0:T(4,128)}, u32[]{:S(2)}) copy-start(s32[1,1,4,384]{3,2,1,0:T(4,128)} %param.12) | copy-start | bytes 18436
  7.2 245.3 %all-reduce.6.cloned.1.call-start = ((), (), s32[]{:S(2)}) async-start(), calls=%async_computation.2 | async-start | bytes 1048576 | tf_op jit(solution)/shard_map/psum | solution.py:30
  8.7 13.2 %collective-permute-start.3 = (f32[384,256]{1,0:T(8,128)S(1)}, f32[384,256]{1,0:T(8,128)S(1)}, u32[]{:S(2)}, u32[]{:S(2)}) collective-permute-start(f32[384,256]{1,0:T(8,128)S(1)} %get-tuple-element.27), channel_id=1, source_target_pairs={{1,0},{2,1},{3,2},{4,3},{5,4},{6,5},{7,6},{8,7},{9,8},{10,9},{11,1... | collective-permute-start | bytes 1179656 | tf_op jit(solution)/shard_map/ppermute | solution.py:12
  10.0 12.8 %collective-permute-start.2 = (f32[384,256]{1,0:T(8,128)S(1)}, f32[384,256]{1,0:T(8,128)S(1)}, u32[]{:S(2)}, u32[]{:S(2)}) collective-permute-start(f32[384,256]{1,0:T(8,128)S(1)} %get-tuple-element.28), channel_id=1, source_target_pairs={{0,1},{1,2},{2,3},{3,4},{4,5},{5,6},{6,7},{7,8},{8,9},{9,10},{10,1... | collective-permute-start | bytes 1179656 | tf_op jit(solution)/shard_map/ppermute | solution.py:12
  15.0 9.6 %collective-permute-start.1 = (f32[384,256]{1,0:T(8,128)S(1)}, f32[384,256]{1,0:T(8,128)S(1)}, u32[]{:S(2)}, u32[]{:S(2)}) collective-permute-start(f32[384,256]{1,0:T(8,128)S(1)} %get-tuple-element.29), channel_id=1, source_target_pairs={{16,0},{32,16},{48,32},{64,48},{80,64},{96,80},{112,96},{17,1},{33... | collective-permute-start | bytes 1179656 | tf_op jit(solution)/shard_map/ppermute | solution.py:12
  17.9 7.9 collective-permute-start
  38.6 11.8 %copy-start.7 = (f32[1536,256]{1,0:T(8,128)}, f32[1536,256]{1,0:T(8,128)S(1)}, u32[]{:S(2)}) copy-start(f32[1536,256]{1,0:T(8,128)S(1)} %gather_fusion) | copy-start | bytes 4718596
  52.1 16.6 %collective-permute-start.7 = (f32[384,256]{0,1:T(8,128)}, f32[384,256]{0,1:T(8,128)}, u32[]{:S(2)}, u32[]{:S(2)}) collective-permute-start(f32[384,256]{0,1:T(8,128)} %get-tuple-element.23), channel_id=1, source_target_pairs={{1,0},{2,1},{3,2},{4,3},{5,4},{6,5},{7,6},{8,7},{9,8},{10,9},{11,1... | collective-permute-start | bytes 1179656 | tf_op jit(solution)/shard_map/ppermute | solution.py:12
  53.4 15.3 %collective-permute-start.6 = (f32[384,256]{0,1:T(8,128)}, f32[384,256]{0,1:T(8,128)}, u32[]{:S(2)}, u32[]{:S(2)}) collective-permute-start(f32[384,256]{0,1:T(8,128)} %get-tuple-element.24), channel_id=1, source_target_pairs={{0,1},{1,2},{2,3},{3,4},{4,5},{5,6},{6,7},{7,8},{8,9},{9,10},{10,1... | collective-permute-start | bytes 1179656 | tf_op jit(solution)/shard_map/ppermute | solution.py:12
  58.3 10.5 %collective-permute-start.5 = (f32[384,256]{0,1:T(8,128)}, f32[384,256]{0,1:T(8,128)}, u32[]{:S(2)}, u32[]{:S(2)}) collective-permute-start(f32[384,256]{0,1:T(8,128)} %get-tuple-element.25), channel_id=1, source_target_pairs={{16,0},{32,16},{48,32},{64,48},{80,64},{96,80},{112,96},{17,1},{33... | collective-permute-start | bytes 1179656 | tf_op jit(solution)/shard_map/ppermute | solution.py:12
  60.2 6.8 copy-start.8
  60.2 9.9 %collective-permute-start.4 = (f32[384,256]{0,1:T(8,128)}, f32[384,256]{0,1:T(8,128)}, u32[]{:S(2)}, u32[]{:S(2)}) collective-permute-start(f32[384,256]{0,1:T(8,128)} %get-tuple-element.22), channel_id=1, source_target_pairs={{0,16},{16,32},{32,48},{48,64},{64,80},{80,96},{96,112},{1,17},{17... | collective-permute-start | bytes 1179656 | tf_op jit(solution)/shard_map/ppermute | solution.py:12
  67.0 28.6 %copy-start.3 = (f32[1,1,1536,256]{2,3,1,0:T(8,128)}, f32[1,1,1536,256]{2,3,1,0:T(8,128)S(1)}, u32[]{:S(2)}) copy-start(f32[1,1,1536,256]{2,3,1,0:T(8,128)S(1)} %copy.11) | copy-start | bytes 4718596
  98.6 153.9 %copy-start.15 = (f32[4,512]{1,0:T(4,128)S(1)}, f32[4,512]{1,0:T(4,128)}, u32[]{:S(2)}) copy-start(f32[4,512]{1,0:T(4,128)} %param.13) | copy-start | bytes 24580
  254.8 20.3 %all-to-all-start = ((f32[128,4,256]{2,1,0:T(4,128)}), f32[128,4,256]{2,1,0:T(4,128)}, u32[]{:S(2)}, u32[]{:S(2)}) async-start(f32[128,4,256]{2,1,0:T(4,128)} %stack.79), calls=%async_computation | async-start | bytes 1048576 | tf_op jit(solution)/shard_map/all_to_all | solution.py:33
  262.0 382.1 %all-reduce.8.cloned.1.call-start = ((), (), s32[]{:S(2)}) async-start(), calls=%async_computation.3 | async-start | bytes 1048576 | tf_op jit(solution)/shard_map/psum | solution.py:30
  283.2 75.8 %collective-permute-start.11 = (f32[384,256]{0,1:T(8,128)}, f32[384,256]{0,1:T(8,128)S(1)}, u32[]{:S(2)}, u32[]{:S(2)}) collective-permute-start(f32[384,256]{0,1:T(8,128)} %get-tuple-element.19), channel_id=1, source_target_pairs={{1,0},{2,1},{3,2},{4,3},{5,4},{6,5},{7,6},{8,7},{9,8},{10,9},{11,1... | collective-permute-start | bytes 1179656 | tf_op jit(solution)/shard_map/ppermute | solution.py:12
  284.4 74.5 %collective-permute-start.10 = (f32[384,256]{0,1:T(8,128)}, f32[384,256]{0,1:T(8,128)S(1)}, u32[]{:S(2)}, u32[]{:S(2)}) collective-permute-start(f32[384,256]{0,1:T(8,128)} %get-tuple-element.20), channel_id=1, source_target_pairs={{0,1},{1,2},{2,3},{3,4},{4,5},{5,6},{6,7},{7,8},{8,9},{9,10},{10,1... | collective-permute-start | bytes 1179656 | tf_op jit(solution)/shard_map/ppermute | solution.py:12
  288.5 70.5 %collective-permute-start.9 = (f32[384,256]{0,1:T(8,128)S(1)}, f32[384,256]{0,1:T(8,128)}, u32[]{:S(2)}, u32[]{:S(2)}) collective-permute-start(f32[384,256]{0,1:T(8,128)S(1)} %get-tuple-element.21), channel_id=1, source_target_pairs={{16,0},{32,16},{48,32},{64,48},{80,64},{96,80},{112,96},{17,1},{33... | collective-permute-start | bytes 1179656 | tf_op jit(solution)/shard_map/ppermute | solution.py:12
  292.2 66.8 %collective-permute-start.8 = (f32[384,256]{0,1:T(8,128)S(1)}, f32[384,256]{0,1:T(8,128)}, u32[]{:S(2)}, u32[]{:S(2)}) collective-permute-start(f32[384,256]{0,1:T(8,128)S(1)} %get-tuple-element.18), channel_id=1, source_target_pairs={{0,16},{16,32},{32,48},{48,64},{64,80},{80,96},{96,112},{1,17},{17... | collective-permute-start | bytes 1179656 | tf_op jit(solution)/shard_map/ppermute | solution.py:12
  387.2 7.6 copy-start.10
  396.2 76.0 %collective-permute-start.15 = (f32[384,256]{0,1:T(8,128)}, f32[384,256]{0,1:T(8,128)S(1)}, u32[]{:S(2)}, u32[]{:S(2)}) collective-permute-start(f32[384,256]{0,1:T(8,128)} %get-tuple-element.13), channel_id=1, source_target_pairs={{1,0},{2,1},{3,2},{4,3},{5,4},{6,5},{7,6},{8,7},{9,8},{10,9},{11,1... | collective-permute-start | bytes 1179656 | tf_op jit(solution)/shard_map/ppermute | solution.py:12
  397.5 74.7 %collective-permute-start.14 = (f32[384,256]{0,1:T(8,128)}, f32[384,256]{0,1:T(8,128)S(1)}, u32[]{:S(2)}, u32[]{:S(2)}) collective-permute-start(f32[384,256]{0,1:T(8,128)} %get-tuple-element.14), channel_id=1, source_target_pairs={{0,1},{1,2},{2,3},{3,4},{4,5},{5,6},{6,7},{7,8},{8,9},{9,10},{10,1... | collective-permute-start | bytes 1179656 | tf_op jit(solution)/shard_map/ppermute | solution.py:12
  401.5 70.7 %collective-permute-start.13 = (f32[384,256]{0,1:T(8,128)S(1)}, f32[384,256]{0,1:T(8,128)}, u32[]{:S(2)}, u32[]{:S(2)}) collective-permute-start(f32[384,256]{0,1:T(8,128)S(1)} %get-tuple-element.15), channel_id=1, source_target_pairs={{16,0},{32,16},{48,32},{64,48},{80,64},{96,80},{112,96},{17,1},{33... | collective-permute-start | bytes 1179656 | tf_op jit(solution)/shard_map/ppermute | solution.py:12
  404.9 67.3 %collective-permute-start.12 = (f32[384,256]{0,1:T(8,128)S(1)}, f32[384,256]{0,1:T(8,128)}, u32[]{:S(2)}, u32[]{:S(2)}) collective-permute-start(f32[384,256]{0,1:T(8,128)S(1)} %get-tuple-element.12), channel_id=1, source_target_pairs={{0,16},{16,32},{32,48},{48,64},{64,80},{80,96},{96,112},{1,17},{17... | collective-permute-start | bytes 1179656 | tf_op jit(solution)/shard_map/ppermute | solution.py:12
  499.8 172.5 %copy-start.1 = (f32[1536,256]{0,1:T(8,128)}, f32[1536,256]{0,1:T(8,128)S(1)}, u32[]{:S(2)}) copy-start(f32[1536,256]{0,1:T(8,128)S(1)} %multiply_add_fusion) | copy-start | bytes 4718596
  646.4 20.3 %all-to-all-start.1 = ((f32[128,4,256]{2,1,0:T(4,128)}), f32[128,4,256]{2,1,0:T(4,128)}, u32[]{:S(2)}, u32[]{:S(2)}) async-start(f32[128,4,256]{2,1,0:T(4,128)} %stack.90), calls=%async_computation.1 | async-start | bytes 1048576 | tf_op jit(solution)/shard_map/all_to_all | solution.py:33
  676.1 76.1 %collective-permute-start.19 = (f32[384,256]{0,1:T(8,128)}, f32[384,256]{0,1:T(8,128)S(1)}, u32[]{:S(2)}, u32[]{:S(2)}) collective-permute-start(f32[384,256]{0,1:T(8,128)} %get-tuple-element.9), channel_id=1, source_target_pairs={{1,0},{2,1},{3,2},{4,3},{5,4},{6,5},{7,6},{8,7},{9,8},{10,9},{11,1... | collective-permute-start | bytes 1179656 | tf_op jit(solution)/shard_map/ppermute | solution.py:12
  677.4 74.8 %collective-permute-start.18 = (f32[384,256]{0,1:T(8,128)}, f32[384,256]{0,1:T(8,128)S(1)}, u32[]{:S(2)}, u32[]{:S(2)}) collective-permute-start(f32[384,256]{0,1:T(8,128)} %get-tuple-element.10), channel_id=1, source_target_pairs={{0,1},{1,2},{2,3},{3,4},{4,5},{5,6},{6,7},{7,8},{8,9},{9,10},{10,1... | collective-permute-start | bytes 1179656 | tf_op jit(solution)/shard_map/ppermute | solution.py:12
  681.4 70.8 %collective-permute-start.17 = (f32[384,256]{0,1:T(8,128)S(1)}, f32[384,256]{0,1:T(8,128)}, u32[]{:S(2)}, u32[]{:S(2)}) collective-permute-start(f32[384,256]{0,1:T(8,128)S(1)} %get-tuple-element.11), channel_id=1, source_target_pairs={{16,0},{32,16},{48,32},{64,48},{80,64},{96,80},{112,96},{17,1},{33... | collective-permute-start | bytes 1179656 | tf_op jit(solution)/shard_map/ppermute | solution.py:12
  685.2 67.1 %collective-permute-start.16 = (f32[384,256]{0,1:T(8,128)S(1)}, f32[384,256]{0,1:T(8,128)}, u32[]{:S(2)}, u32[]{:S(2)}) collective-permute-start(f32[384,256]{0,1:T(8,128)S(1)} %get-tuple-element.8), channel_id=1, source_target_pairs={{0,16},{16,32},{32,48},{48,64},{64,80},{80,96},{96,112},{1,17},{17... | collective-permute-start | bytes 1179656 | tf_op jit(solution)/shard_map/ppermute | solution.py:12
  (10 other events, 18.0 us)
Sparse Core Ops, SparseCore 0:
  100.7 151.7 all-reduce.5
  501.8 142.2 all-reduce.7
